TPU v7x, 32 devices: a whole 2x2x4 slice. The times are simulated.
32 devices in a mesh: groups: 2 (over y), row: 4 (over z), col: 2 (over x), sub: 2 (over core).
Axes of the slice: x: 2, y: 2, z: 4, core: 2. Of those that a mesh axis runs over, the one named last changes fastest.
Arguments:
- stream_in: bfloat16 [4096, 5376], P(('groups', 'row'), ('col', 'sub')), parts along dimension 0, may hold values from -6 to 6
- in_gain: float32 [5376], replicated, may hold values from 0.1 to 1.9
- query_weight: bfloat16 [5376, 4096], P('row', ('col', 'sub')), may hold values from -0.078125 to 0.078125
- key_matrix: bfloat16 [5376, 2048], P('row', ('col', 'sub')), may hold values from -0.078125 to 0.078125
- value_matrix: bfloat16 [5376, 2048], P('row', ('col', 'sub')), may hold values from -0.078125 to 0.078125
- query_gain: float32 [128], replicated, may hold values from 0.45 to 10, as said below
- key_norm_gain: float32 [128], replicated, may hold values from 0.45 to 10, as said below
- output_weight: bfloat16 [4096, 5376], P('row', ('col', 'sub')), may hold values from -3 to 3
- post_gain: float32 [5376], P(('col', 'sub')), may hold values from 0.1 to 1.9
Outputs:
- stream_out: bfloat16 [4096, 5376], P(('groups', 'row'), ('col', 'sub')), parts along dimension 0
There are 2 independent parts, one for each index of `groups`. A program takes and returns all parts, laid end to end along the dimension named above; an argument that names none is the same for every part. Nothing has to cross between parts.
Inputs may be any that keep to these rules, and one draw needn't show every extreme that they name: `query_gain`: positive. `key_norm_gain`: positive.
All inputs are finite; a program needn't handle non-finite values.
Results may differ from a plain program's by a relative error of at most 0.014.
The roundings to bfloat16 on the way count: a program that leaves them out, or rounds other values in their place, can miss the bound.
Values may be sent and summed in bfloat16 or wider, within the bound.
A program may use at most 128 MiB of HBM per device.

v0:
```python
import jax
import jax.numpy as jnp
from jax import lax
from jax.sharding import PartitionSpec as P

MODEL_WIDTH = 5376
QUERY_HEAD_COUNT = 32
WINDOW_LENGTH = 1024
EPSILON = 1e-06


def shifted(x, axis, by):
    count = lax.axis_size(axis)
    pairs = [(i, i + by) for i in range(count) if 0 <= i + by < count]
    return lax.ppermute(x, axis, pairs)


def root_mean_scale(values, gain):
    return values * lax.rsqrt(jnp.mean(values * values, axis=-1, keepdims=True) + EPSILON) * gain


def apply_rotary(tensor, token_positions):
    half_dim = tensor.shape[-1] // 2
    inverse = 10000.0 ** (-(jnp.arange(half_dim, dtype=jnp.float32) * 2.0) / tensor.shape[-1])
    angles = token_positions[:, None] * inverse[None, :]
    cosine = jnp.cos(angles)[:, None, :]
    sine_part = jnp.sin(angles)[:, None, :]
    first_half = tensor[..., :half_dim]
    second_half = tensor[..., half_dim:]
    return jnp.concatenate(
        [
            first_half * cosine - second_half * sine_part,
            second_half * cosine + first_half * sine_part,
        ],
        axis=-1,
    )


def on_device(
    stream_in,
    in_gain,
    query_weight,
    key_matrix,
    value_matrix,
    query_gain,
    key_norm_gain,
    output_weight,
    post_gain,
):
    token_rows = lax.all_gather(stream_in, ("col", "sub"), axis=1, tiled=True)
    tokens = token_rows.shape[0]
    normed = root_mean_scale(token_rows.astype(jnp.float32), in_gain).astype(jnp.bfloat16)

    def add_panel(panel_piece):
        return jnp.dot(normed, panel_piece, preferred_element_type=jnp.float32)

    query_proj = add_panel(lax.all_gather(query_weight, "row", axis=0, tiled=True))
    projected_keys = add_panel(lax.all_gather(key_matrix, "row", axis=0, tiled=True))
    projected_values = add_panel(lax.all_gather(value_matrix, "row", axis=0, tiled=True))
    head_size = query_gain.shape[0]
    query_heads = query_weight.shape[1] // head_size
    pair_heads = key_matrix.shape[1] // head_size
    group_count = query_heads // pair_heads
    scale_factor = float(MODEL_WIDTH // QUERY_HEAD_COUNT) ** (-0.5)
    row_index = lax.axis_index("row")
    query_places = row_index * tokens + jnp.arange(tokens, dtype=jnp.int32)
    query_rot = apply_rotary(
        root_mean_scale(query_proj.reshape(tokens, query_heads, head_size), query_gain),
        query_places.astype(jnp.float32),
    ).astype(jnp.bfloat16)
    rotary_keys = apply_rotary(
        root_mean_scale(projected_keys.reshape(tokens, pair_heads, head_size), key_norm_gain),
        query_places.astype(jnp.float32),
    ).astype(jnp.bfloat16)
    keys_flat = rotary_keys.reshape(tokens, pair_heads * head_size)
    values_flat = projected_values.astype(jnp.bfloat16)
    shards_back = min(WINDOW_LENGTH // tokens, lax.axis_size("row") - 1)
    band_length = (shards_back + 1) * tokens
    key_parts = [keys_flat]
    value_parts = [values_flat]
    for offset in range(1, shards_back + 1):
        keys_prior, values_prior = shifted((keys_flat, values_flat), "row", offset)
        key_parts = [keys_prior] + key_parts
        value_parts = [values_prior] + value_parts
    keys_band = jnp.concatenate(key_parts, axis=0)
    values_band = jnp.concatenate(value_parts, axis=0)
    key_places = (row_index - shards_back) * tokens + jnp.arange(band_length, dtype=jnp.int32)
    distance = query_places[:, None] - key_places[None, :]
    visible = (distance >= 0) & (distance < WINDOW_LENGTH) & (key_places[None, :] >= 0)
    grouped = query_rot.reshape(tokens, pair_heads, group_count, head_size)
    scores = (
        jnp.einsum(
            "qhgd,shd->hgqs",
            grouped,
            keys_band.reshape(band_length, pair_heads, head_size),
            preferred_element_type=jnp.float32,
        )
        * scale_factor
    )
    scores = jnp.where(visible, scores, -1e30)
    row_max = jnp.max(scores, axis=-1, keepdims=True)
    exponent = jnp.exp(scores - row_max)
    weights = (exponent / jnp.sum(exponent, axis=-1, keepdims=True)).astype(jnp.bfloat16)
    attended = jnp.einsum(
        "hgqs,shd->qhgd",
        weights,
        values_band.reshape(band_length, pair_heads, head_size),
        preferred_element_type=jnp.float32,
    )
    heads_out = attended.reshape(tokens, query_heads * head_size).astype(jnp.bfloat16)
    head_rows = lax.all_gather(heads_out, ("col", "sub"), axis=1, tiled=True)
    branch = jnp.dot(
        head_rows,
        lax.all_gather(output_weight, "row", axis=0, tiled=True),
        preferred_element_type=jnp.float32,
    )
    squares = lax.psum(jnp.sum(branch * branch, axis=-1), ("col", "sub"))
    scaled = branch * lax.rsqrt(squares[:, None] / MODEL_WIDTH + EPSILON) * post_gain
    return (stream_in.astype(jnp.float32) + scaled).astype(jnp.bfloat16)


def solution(mesh):
    placed = (
        P(("groups", "row"), ("col", "sub")),
        P(),
        P("row", ("col", "sub")),
        P("row", ("col", "sub")),
        P("row", ("col", "sub")),
        P(),
        P(),
        P("row", ("col", "sub")),
        P(("col", "sub")),
    )
    return jax.shard_map(
        on_device,
        mesh=mesh,
        in_specs=placed,
        out_specs=P(("groups", "row"), ("col", "sub")),
        check_vma=False,
    )
```

profile of v0, /device:TPU:0, one launch (start us, length us, event | category | flops | bytes accessed | tf_op | source)
XLA Modules:
  0.0 759.0 jit_solution(18262040499544532429)
XLA Ops:
  11.0 42.5 %all-gather.7.cloned.1.call-done = bf16[512,5376]{0,1:T(8,128)(2,1)} async-done(((bf16[512,1344]{0,1:T(8,128)(2,1)}), bf16[512,5376]{0,1:T(8,128)(2,1)}) %all-gather.7.cloned.1.call-update) | async-done | bytes 5505040 | tf_op jit(solution)/shard_map/all_gather | solution.py:50
  53.5 3.8 fusion.6
  57.3 100.2 %all-gather.11.cloned.1.call-done = bf16[5376,512]{1,0:T(8,128)(2,1)} async-done(((bf16[1344,512]{1,0:T(8,128)(2,1)}), bf16[5376,512]{1,0:T(8,128)(2,1)}) %all-gather.11.cloned.1.call-update) | async-done | bytes 5505040 | tf_op jit(solution)/shard_map/all_gather | solution.py:58
  157.5 7.6 %multiply_reduce_fusion.2 = (f32[512,4]{0,1:T(4,128)S(1)}, f32[512,512]{0,1:T(8,128)S(1)}) fusion(bf16[5376,512]{1,0:T(8,128)(2,1)} %all-gather.11.cloned.1.call-done, bf16[512,5376]{0,1:T(8,128)(2,1)} %all-gather.7.cloned.1.call-done, f32[5376]{0:T(1024)S(1)} %copy-done.6, f32[512]{0:T(512)S(1)} %add_rsqrt_fusion.3), kind=kOutput, calls=%fused_computation.35 | convolution fusion | flops 2830104576 | bytes 12090368 | tf_op jit(solution)/shard_map/dot_general | solution.py:55
  166.8 2.7 collective-permute-start.2
  169.4 2.2 collective-permute-start.3
  171.6 106.4 %all-gather.9.cloned.1.call-done = bf16[5376,512]{1,0:T(8,128)(2,1)} async-done(((bf16[1344,512]{1,0:T(8,128)(2,1)}), bf16[5376,512]{1,0:T(8,128)(2,1)}) %all-gather.9.cloned.1.call-update) | async-done | bytes 5505040 | tf_op jit(solution)/shard_map/all_gather | solution.py:59
  278.1 7.4 convolution_convert_fusion
  285.4 5.1 collective-permute-start
  290.6 16.2 %collective-permute-start.1 = (bf16[512,512]{1,0:T(8,128)(2,1)S(1)}, bf16[512,512]{1,0:T(8,128)(2,1)}, u32[]{:S(2)}, u32[]{:S(2)}) collective-permute-start(bf16[512,512]{1,0:T(8,128)(2,1)S(1)} %convolution_convert_fusion), channel_id=1, source_target_pairs={{0,4},{4,8},{8,12},{1,5},{5,9},{9,13},{2,6},{6,10},{10,14},{3,7},{... | collective-permute-start | bytes 1572872 | tf_op jit(solution)/shard_map/ppermute | solution.py:15
  306.8 1.9 fusion.12
  310.7 18.4 %collective-permute-done.1 = bf16[512,512]{1,0:T(8,128)(2,1)} collective-permute-done((bf16[512,512]{1,0:T(8,128)(2,1)S(1)}, bf16[512,512]{1,0:T(8,128)(2,1)}, u32[]{:S(2)}, u32[]{:S(2)}) %collective-permute-start.1) | collective-permute-done | bytes 524320 | tf_op jit(solution)/shard_map/ppermute | solution.py:15
  329.1 1.3 pad_maximum_fusion
  330.5 1.6 copy.45
  332.1 160.1 %all-gather.13.cloned.1.call-done = bf16[5376,1024]{1,0:T(8,128)(2,1)} async-done(((bf16[1344,1024]{1,0:T(8,128)(2,1)}), bf16[5376,1024]{1,0:T(8,128)(2,1)}) %all-gather.13.cloned.1.call-update) | async-done | bytes 11010064 | tf_op jit(solution)/shard_map/all_gather | solution.py:57
  492.2 11.7 %convolution_bitcast_fusion = f32[64,8,8,128]{3,1,2,0:T(8,128)S(1)} fusion(bf16[5376,1024]{1,0:T(8,128)(2,1)} %all-gather.13.cloned.1.call-done, bf16[512,5376]{0,1:T(8,128)(2,1)} %all-gather.7.cloned.1.call-done, f32[5376]{0:T(1024)S(1)} %copy-done.6, f32[512]{0:T(512)S(1)} %add_rsqrt_fusion.3), kind=kOutput, calls=%fused_computation.25 | convolution fusion | flops 5648154624 | bytes 18635776 | tf_op jit(solution)/shard_map/dot_general | solution.py:55
  508.4 14.3 %fusion.14 = f32[4,1536,512,2]{2,1,3,0:T(8,128)} fusion(bf16[512,4,128]{2,0,1:T(8,128)(2,1)S(1)} %maximum_convert_fusion, bf16[512,4,128]{2,0,1:T(8,128)(2,1)S(1)} %copy-done.2, bf16[512,4,128]{2,0,1:T(8,128)(2,1)S(1)} %copy-done.1, bf16[512,4,2,64]{3,0,2,1:T(8,128)(2,1)S(1)} %bitcast.48, bf16[512,4,2,64]{3,0,2,1:T(8,128)(2,1)S(1)} %bitcast.50), kind=kOutput, calls=%fused_computation.36 | convolution fusion | flops 1617428480 | bytes 27787264 | tf_op jit(solution)/shard_map/qhgd,shd->hgqs/dot_general | solution.py:92
  522.7 10.5 %fusion.30 = f32[4,2,512]{2,1,0:T(2,128)S(1)} fusion(pred[512,1536]{0,1:T(8,128)(4,1)} %fusion.12, bf16[512,4,128]{2,0,1:T(8,128)(2,1)S(1)} %maximum_convert_fusion, bf16[512,4,128]{2,0,1:T(8,128)(2,1)} %copy.35, bf16[512,4,128]{2,0,1:T(8,128)(2,1)S(1)} %copy-done.1, bf16[512,4,2,64]{3,0,2,1:T(8,128)(2,1)S(1)} %bitcast.49, ...), kind=kOutput, calls=%fused_computation.56 | convolution fusion | flops 1642595840 | bytes 3424256 | tf_op jit(solution)/shard_map/sub | solution.py:102
  533.2 15.3 %fusion.13 = bf16[4,128,2,512]{3,1,2,0:T(8,128)(2,1)} fusion(bf16[1536,4,128,1]{0,2,3,1:T(8,128)(2,1)} %bitcast.52, f32[4,2,512]{2,1,0:T(2,128)S(1)} %fusion.30, f32[4,1536,512,2]{2,1,3,0:T(8,128)} %fusion.14, pred[512,1536]{0,1:T(8,128)(4,1)} %fusion.12), kind=kOutput, calls=%fused_computation.28 | convolution fusion | flops 1642599936 | bytes 28590080 | tf_op jit(solution)/shard_map/hgqs,shd->qhgd/dot_general | solution.py:104
  548.5 149.4 %all-gather.17.cloned.1.call-done = bf16[4096,1344]{0,1:T(8,128)(2,1)} async-done(((bf16[1024,1344]{0,1:T(8,128)(2,1)}), bf16[4096,1344]{0,1:T(8,128)(2,1)}) %all-gather.17.cloned.1.call-update) | async-done | bytes 11010064 | tf_op jit(solution)/shard_map/all_gather | solution.py:114
  697.9 34.1 %all-gather.15.cloned.1.call-done = bf16[512,4096]{0,1:T(8,128)(2,1)} async-done(((bf16[512,1024]{0,1:T(8,128)(2,1)}), bf16[512,4096]{0,1:T(8,128)(2,1)}) %all-gather.15.cloned.1.call-update) | async-done | bytes 4194320 | tf_op jit(solution)/shard_map/all_gather | solution.py:111
  732.0 10.9 %multiply_reduce_fusion = (f32[512]{0:T(512)S(1)}, f32[512,1344]{0,1:T(8,128)}) fusion(bf16[4096,1344]{0,1:T(8,128)(2,1)} %all-gather.17.cloned.1.call-done, bf16[512,4096]{0,1:T(8,128)(2,1)} %all-gather.15.cloned.1.call-done), kind=kOutput, calls=%fused_computation.20 | convolution fusion | flops 5638520320 | bytes 17958912 | tf_op jit(solution)/shard_map/dot_general | solution.py:112
  742.9 5.9 psum.7
  748.8 3.3 add_convert_fusion
  (54 shorter events, 12.5 us)
Async XLA Ops:
  6.5 47.0 %all-gather.7.cloned.1.call-start = ((), (), s32[]{:S(2)}) async-start(), calls=%async_computation | async-start | bytes 6881280 | tf_op jit(solution)/shard_map/all_gather | solution.py:50
  7.3 150.2 %all-gather.11.cloned.1.call-start = ((), (), s32[]{:S(2)}) async-start(), calls=%async_computation.2 | async-start | bytes 6881280 | tf_op jit(solution)/shard_map/all_gather | solution.py:58
  8.0 270.0 %all-gather.9.cloned.1.call-start = ((), (), s32[]{:S(2)}) async-start(), calls=%async_computation.1 | async-start | bytes 6881280 | tf_op jit(solution)/shard_map/all_gather | solution.py:59
  8.7 483.4 %all-gather.13.cloned.1.call-start = ((), (), s32[]{:S(2)}) async-start(), calls=%async_computation.3 | async-start | bytes 13762560 | tf_op jit(solution)/shard_map/all_gather | solution.py:57
  9.3 688.6 %all-gather.17.cloned.1.call-start = ((), (), s32[]{:S(2)}) async-start(), calls=%async_computation.5 | async-start | bytes 13762560 | tf_op jit(solution)/shard_map/all_gather | solution.py:114
  9.9 147.6 %copy-start.6 = (f32[5376]{0:T(1024)S(1)}, f32[5376]{0:T(1024)}, u32[]{:S(2)}) copy-start(f32[5376]{0:T(1024)} %param.10) | copy-start | bytes 64516
  9.9 722.1 %all-gather.15.cloned.1.call-start = ((), (), s32[]{:S(2)}) async-start(), calls=%async_computation.4 | async-start | bytes 5242880 | tf_op jit(solution)/shard_map/all_gather | solution.py:111
  57.3 108.2 %copy-start.4 = (f32[128]{0:T(128)S(1)}, f32[128]{0:T(128)}, u32[]{:S(2)}) copy-start(f32[128]{0:T(128)} %param.15) | copy-start | bytes 1540
  166.8 141.9 %collective-permute-start.2 = (bf16[512,512]{0,1:T(8,128)(2,1)S(1)}, bf16[512,512]{0,1:T(8,128)(2,1)S(1)}, u32[]{:S(2)}, u32[]{:S(2)}) collective-permute-start(bf16[512,512]{0,1:T(8,128)(2,1)S(1)} %bitcast.55), channel_id=1, source_target_pairs={{0,8},{4,12},{1,9},{5,13},{2,10},{6,14},{3,11},{7,15},{16,24},{20,... | collective-permute-start | bytes 1572872 | tf_op jit(solution)/shard_map/ppermute | solution.py:15
  169.4 140.3 %collective-permute-start.3 = (bf16[512,512]{0,1:T(8,128)(2,1)S(1)}, bf16[512,512]{0,1:T(8,128)(2,1)S(1)}, u32[]{:S(2)}, u32[]{:S(2)}) collective-permute-start(bf16[512,512]{0,1:T(8,128)(2,1)S(1)} %bitcast.56), channel_id=1, source_target_pairs={{0,4},{4,8},{8,12},{1,5},{5,9},{9,13},{2,6},{6,10},{10,14},{3,7},{... | collective-permute-start | bytes 1572872 | tf_op jit(solution)/shard_map/ppermute | solution.py:15
  285.4 25.3 %collective-permute-start = (bf16[512,512]{1,0:T(8,128)(2,1)S(1)}, bf16[512,512]{1,0:T(8,128)(2,1)}, u32[]{:S(2)}, u32[]{:S(2)}) collective-permute-start(bf16[512,512]{1,0:T(8,128)(2,1)S(1)} %convolution_convert_fusion), channel_id=1, source_target_pairs={{0,8},{4,12},{1,9},{5,13},{2,10},{6,14},{3,11},{7,15},{16,24},{20,... | collective-permute-start | bytes 1572872 | tf_op jit(solution)/shard_map/ppermute | solution.py:15
  290.6 38.6 %collective-permute-start.1 = (bf16[512,512]{1,0:T(8,128)(2,1)S(1)}, bf16[512,512]{1,0:T(8,128)(2,1)}, u32[]{:S(2)}, u32[]{:S(2)}) collective-permute-start(bf16[512,512]{1,0:T(8,128)(2,1)S(1)} %convolution_convert_fusion), channel_id=1, source_target_pairs={{0,4},{4,8},{8,12},{1,5},{5,9},{9,13},{2,6},{6,10},{10,14},{3,7},{... | collective-permute-start | bytes 1572872 | tf_op jit(solution)/shard_map/ppermute | solution.py:15
  503.9 1.4 copy-start.5
  507.2 1.0 copy-start.1
  507.2 1.2 copy-start.2
  548.5 200.3 %copy-start = (bf16[512,1344]{0,1:T(8,128)(2,1)S(1)}, bf16[512,1344]{0,1:T(8,128)(2,1)}, u32[]{:S(2)}) copy-start(bf16[512,1344]{0,1:T(8,128)(2,1)} %param.9) | copy-start | bytes 4128772
  548.5 200.3 %copy-start.3 = (f32[1344]{0:T(1024)S(1)}, f32[1344]{0:T(1024)}, u32[]{:S(2)}) copy-start(f32[1344]{0:T(1024)} %param.17) | copy-start | bytes 16132
Sparse Core Ops, SparseCore 0:
  8.9 44.6 all-gather.6
  55.1 102.3 all-gather.10
  159.1 118.9 all-gather.8
  279.5 212.6 all-gather.12
  493.6 204.2 all-gather.16
  699.3 32.6 all-gather.14
where the time goes:
time: 759 us
  waiting for transfers between devices  614 us (81%)
  matrix products  77.7 us (10%)
  starting transfers between devices  26.3 us (3%)
  other arithmetic  15 us (2%)
  between operations  13.7 us (2%)
    all_gather x1, waiting for transfers between devices, on_device(): lax.all_gather(query_weight, 'row', axis=0, tiled=True)  160 us
    all_gather x1, waiting for transfers between devices, on_device(): lax.all_gather(output_weight, 'row', axis=0, tiled=True)  149 us
    all_gather x1, waiting for transfers between devices, on_device(): lax.all_gather(value_matrix, 'row', axis=0, tiled=True)  106 us
    all_gather x1, waiting for transfers between devices, on_device(): lax.all_gather(key_matrix, 'row', axis=0, tiled=True)  100 us
    all_gather x1, waiting for transfers between devices, on_device(): token_rows = lax.all_gather(stream_in, ('col', 'sub'), axis=1, tiled=True)  42.5 us
    all_gather x1, waiting for transfers between devices, on_device(): head_rows = lax.all_gather(heads_out, ('col', 'sub'), axis=1, tiled=True)  34.1 us
    dot_general x3, matrix products, add_panel(): return jnp.dot(normed, panel_piece, preferred_element_type=jnp.float32)  26.7 us
    ppermute x4, starting transfers between devices, shifted(): return lax.ppermute(x, axis, pairs)  26.1 us
  transfers between devices with their start and end apart: 10, of which 7 were waited for; matrix products, arithmetic and copies ran while one was open for 11% of the time, Pallas kernels for 0%

commit v1 on v0

--- a/solution.py
+++ b/solution.py
@@ -7,6 +7,19 @@
 QUERY_HEAD_COUNT = 32
 WINDOW_LENGTH = 1024
 EPSILON = 1e-06
+
+
+def collect(array, axis, dim):
+    size, index, width = (lax.axis_size(axis), lax.axis_index(axis), array.shape[dim])
+    upward = [(i, (i + 1) % size) for i in range(size)]
+    filled = jnp.zeros((*array.shape[:dim], size * width, *array.shape[dim + 1 :]), array.dtype)
+    block = array
+    for hop in range(size):
+        holder = (index - hop) % size
+        filled = lax.dynamic_update_slice_in_dim(filled, block, holder * width, axis=dim)
+        if hop < size - 1:
+            block = lax.ppermute(block, axis, upward)
+    return filled
 
 
 def shifted(x, axis, by):
@@ -110,9 +123,7 @@
     heads_out = attended.reshape(tokens, query_heads * head_size).astype(jnp.bfloat16)
     head_rows = lax.all_gather(heads_out, ("col", "sub"), axis=1, tiled=True)
     branch = jnp.dot(
-        head_rows,
-        lax.all_gather(output_weight, "row", axis=0, tiled=True),
-        preferred_element_type=jnp.float32,
+        head_rows, collect(output_weight, "row", 0), preferred_element_type=jnp.float32
     )
     squares = lax.psum(jnp.sum(branch * branch, axis=-1), ("col", "sub"))
     scaled = branch * lax.rsqrt(squares[:, None] / MODEL_WIDTH + EPSILON) * post_gain

time: 759 us -> 729 us (0.960); the launches traced: 759 us -> 720 us
  waiting for transfers between devices: 614 us -> 545 us
  local copies, waits for them, and re-layouts: 6.05 us -> 24.4 us
  starting transfers between devices: 26.3 us -> 42 us
    all_gather x1 -> x0, waiting for transfers between devices: 149 us -> none  [on_device(): lax.all_gather(output_weight, 'row', axis=0, tiled=True)]
    ppermute x0 -> x3, waiting for transfers between devices: none -> 111 us  [collect(): block = lax.ppermute(block, axis, upward)]
    all_gather x1, waiting for transfers between devices: 34.1 us -> 0.01 us  [on_device(): head_rows = lax.all_gather(heads_out, ('col', 'sub'), axis=1, tiled=True)]
    ppermute x0 -> x3, starting transfers between devices: none -> 14.2 us  [collect(): block = lax.ppermute(block, axis, upward)]
    dynamic_update_slice x0 -> x4, local copies, waits for them, and re-layouts: none -> 12.8 us  [collect(): lax.dynamic_update_slice_in_dim(filled, block, holder * width, axis=dim)]
  transfers between devices with their start and end apart: 10 -> 12, of which waited for: 7 -> 7; matrix products, arithmetic and copies ran while one was open for 11% -> 14% of each run, Pallas kernels for 0% -> 0%
where the time goes in v1:
time: 729 us; the launch traced here: 720 us
  waiting for transfers between devices  545 us (75%)
  matrix products  75.2 us (10%)
  starting transfers between devices  42 us (6%)
  local copies, waits for them, and re-layouts  24.4 us (3%)
  other arithmetic  15 us (2%)
  between operations  13.6 us (2%)
    all_gather x1, waiting for transfers between devices, on_device(): lax.all_gather(query_weight, 'row', axis=0, tiled=True)  160 us
    ppermute x3, waiting for transfers between devices, collect(): block = lax.ppermute(block, axis, upward)  111 us
    all_gather x1, waiting for transfers between devices, on_device(): lax.all_gather(key_matrix, 'row', axis=0, tiled=True)  106 us
    all_gather x1, waiting for transfers between devices, on_device(): lax.all_gather(value_matrix, 'row', axis=0, tiled=True)  106 us
    all_gather x1, waiting for transfers between devices, on_device(): token_rows = lax.all_gather(stream_in, ('col', 'sub'), axis=1, tiled=True)  40 us
    ppermute x4, starting transfers between devices, shifted(): return lax.ppermute(x, axis, pairs)  27.7 us
    dot_general x3, matrix products, add_panel(): return jnp.dot(normed, panel_piece, preferred_element_type=jnp.float32)  26.7 us
    ppermute x4, waiting for transfers between devices, shifted(): return lax.ppermute(x, axis, pairs)  17.9 us
  transfers between devices with their start and end apart: 12, of which 7 were waited for; matrix products, arithmetic and copies ran while one was open for 14% of the time, Pallas kernels for 0%

profile of v1, /device:TPU:0, one launch (start us, length us, event | category | flops | bytes accessed | tf_op | source)
XLA Modules:
  0.0 720.4 jit_solution(6939861807186631846)
XLA Ops:
  13.5 40.0 %all-gather.6.cloned.1.call-done = bf16[512,5376]{0,1:T(8,128)(2,1)} async-done(((bf16[512,1344]{0,1:T(8,128)(2,1)}), bf16[512,5376]{0,1:T(8,128)(2,1)}) %all-gather.6.cloned.1.call-update) | async-done | bytes 5505040 | tf_op jit(solution)/shard_map/all_gather | solution.py:63
  53.5 3.8 fusion.6
  57.3 106.4 %all-gather.10.cloned.1.call-done = bf16[5376,512]{1,0:T(8,128)(2,1)} async-done(((bf16[1344,512]{1,0:T(8,128)(2,1)}), bf16[5376,512]{1,0:T(8,128)(2,1)}) %all-gather.10.cloned.1.call-update) | async-done | bytes 5505040 | tf_op jit(solution)/shard_map/all_gather | solution.py:71
  163.7 7.6 %multiply_reduce_fusion.2 = (f32[512,4]{0,1:T(4,128)S(1)}, f32[512,512]{0,1:T(8,128)S(1)}) fusion(bf16[5376,512]{1,0:T(8,128)(2,1)} %all-gather.10.cloned.1.call-done, bf16[512,5376]{0,1:T(8,128)(2,1)} %all-gather.6.cloned.1.call-done, f32[5376]{0:T(1024)S(1)} %copy-done.6, f32[512]{0:T(512)S(1)} %add_rsqrt_fusion.3), kind=kOutput, calls=%fused_computation.35 | convolution fusion | flops 2830104576 | bytes 12090368 | tf_op jit(solution)/shard_map/dot_general | solution.py:68
  175.5 3.4 collective-permute-start.3
  178.9 106.2 %all-gather.8.cloned.1.call-done = bf16[5376,512]{1,0:T(8,128)(2,1)} async-done(((bf16[1344,512]{1,0:T(8,128)(2,1)}), bf16[5376,512]{1,0:T(8,128)(2,1)}) %all-gather.8.cloned.1.call-update) | async-done | bytes 5505040 | tf_op jit(solution)/shard_map/all_gather | solution.py:72
  285.1 7.4 %convolution_convert_fusion = bf16[512,512]{1,0:T(8,128)(2,1)S(1)} fusion(bf16[5376,512]{1,0:T(8,128)(2,1)} %all-gather.8.cloned.1.call-done, bf16[512,5376]{0,1:T(8,128)(2,1)} %all-gather.6.cloned.1.call-done, f32[5376]{0:T(1024)S(1)} %copy-done.6, f32[512]{0:T(512)S(1)} %add_rsqrt_fusion.3), kind=kOutput, calls=%fused_computation.29 | convolution fusion | flops 2829844480 | bytes 11557888 | tf_op jit(solution)/shard_map/dot_general | solution.py:68
  292.5 5.1 collective-permute-start
  297.6 16.6 %collective-permute-start.1 = (bf16[512,512]{1,0:T(8,128)(2,1)S(1)}, bf16[512,512]{1,0:T(8,128)(2,1)}, u32[]{:S(2)}, u32[]{:S(2)}) collective-permute-start(bf16[512,512]{1,0:T(8,128)(2,1)S(1)} %convolution_convert_fusion), channel_id=1, source_target_pairs={{0,4},{4,8},{8,12},{1,5},{5,9},{9,13},{2,6},{6,10},{10,14},{3,7},{... | collective-permute-start | bytes 1572872 | tf_op jit(solution)/shard_map/ppermute | solution.py:28
  318.3 17.9 %collective-permute-done.1 = bf16[512,512]{1,0:T(8,128)(2,1)} collective-permute-done((bf16[512,512]{1,0:T(8,128)(2,1)S(1)}, bf16[512,512]{1,0:T(8,128)(2,1)}, u32[]{:S(2)}, u32[]{:S(2)}) %collective-permute-start.1) | collective-permute-done | bytes 524320 | tf_op jit(solution)/shard_map/ppermute | solution.py:28
  339.1 160.1 %all-gather.12.cloned.1.call-done = bf16[5376,1024]{1,0:T(8,128)(2,1)} async-done(((bf16[1344,1024]{1,0:T(8,128)(2,1)}), bf16[5376,1024]{1,0:T(8,128)(2,1)}) %all-gather.12.cloned.1.call-update) | async-done | bytes 11010064 | tf_op jit(solution)/shard_map/all_gather | solution.py:70
  499.2 11.7 %convolution_bitcast_fusion = f32[64,8,8,128]{3,1,2,0:T(8,128)S(1)} fusion(bf16[5376,1024]{1,0:T(8,128)(2,1)} %all-gather.12.cloned.1.call-done, bf16[512,5376]{0,1:T(8,128)(2,1)} %all-gather.6.cloned.1.call-done, f32[5376]{0:T(1024)S(1)} %copy-done.6, f32[512]{0:T(512)S(1)} %add_rsqrt_fusion.3), kind=kOutput, calls=%fused_computation.25 | convolution fusion | flops 5648154624 | bytes 18635776 | tf_op jit(solution)/shard_map/dot_general | solution.py:68
  515.4 11.8 %fusion.14 = f32[4,1536,512,2]{2,1,3,0:T(8,128)} fusion(bf16[512,4,128]{2,0,1:T(8,128)(2,1)S(1)} %maximum_convert_fusion, bf16[512,4,128]{2,0,1:T(8,128)(2,1)S(1)} %copy-done.2, bf16[512,4,128]{2,0,1:T(8,128)(2,1)S(1)} %copy-done.1, bf16[512,4,2,64]{3,0,2,1:T(8,128)(2,1)S(1)} %bitcast.48, bf16[512,4,2,64]{3,0,2,1:T(8,128)(2,1)S(1)} %bitcast.50), kind=kOutput, calls=%fused_computation.36 | convolution fusion | flops 1617428480 | bytes 27787264 | tf_op jit(solution)/shard_map/qhgd,shd->hgqs/dot_general | solution.py:105
  527.2 10.5 %fusion.30 = f32[4,2,512]{2,1,0:T(2,128)S(1)} fusion(pred[512,1536]{0,1:T(8,128)(4,1)} %fusion.12, bf16[512,4,128]{2,0,1:T(8,128)(2,1)S(1)} %maximum_convert_fusion, bf16[512,4,128]{2,0,1:T(8,128)(2,1)} %copy.35, bf16[512,4,128]{2,0,1:T(8,128)(2,1)S(1)} %copy-done.1, bf16[512,4,2,64]{3,0,2,1:T(8,128)(2,1)S(1)} %bitcast.49, ...), kind=kOutput, calls=%fused_computation.60 | convolution fusion | flops 1642595840 | bytes 3424256 | tf_op jit(solution)/shard_map/sub | solution.py:115
  537.7 15.2 %fusion.13 = bf16[4,128,2,512]{3,1,2,0:T(8,128)(2,1)} fusion(bf16[1536,4,128,1]{0,2,3,1:T(8,128)(2,1)} %bitcast.52, f32[4,2,512]{2,1,0:T(2,128)S(1)} %fusion.30, f32[4,1536,512,2]{2,1,3,0:T(8,128)} %fusion.14, pred[512,1536]{0,1:T(8,128)(4,1)} %fusion.12), kind=kOutput, calls=%fused_computation.28 | convolution fusion | flops 1642599936 | bytes 28590080 | tf_op jit(solution)/shard_map/hgqs,shd->qhgd/dot_general | solution.py:117
  553.0 11.1 %collective-permute-start.5 = (bf16[1024,1344]{0,1:T(8,128)(2,1)}, bf16[1024,1344]{0,1:T(8,128)(2,1)S(1)}, u32[]{:S(2)}, u32[]{:S(2)}) collective-permute-start(bf16[1024,1344]{0,1:T(8,128)(2,1)} %collective-permute-done.4), channel_id=1, source_target_pairs={{0,4},{4,8},{8,12},{12,0},{1,5},{5,9},{9,13},{13,1},{2,6},{6,10},{... | collective-permute-start | bytes 8257544 | tf_op jit(solution)/shard_map/ppermute | solution.py:21
  564.0 63.1 %collective-permute-done.5 = bf16[1024,1344]{0,1:T(8,128)(2,1)S(1)} collective-permute-done((bf16[1024,1344]{0,1:T(8,128)(2,1)}, bf16[1024,1344]{0,1:T(8,128)(2,1)S(1)}, u32[]{:S(2)}, u32[]{:S(2)}) %collective-permute-start.5) | collective-permute-done | bytes 2752544 | tf_op jit(solution)/shard_map/ppermute | solution.py:21
  627.1 5.6 broadcast_in_dim.10
  632.7 3.6 constant_dynamic-update-slice_fusion.3
  636.3 3.6 constant_dynamic-update-slice_fusion.2
  641.8 48.2 %collective-permute-done.6 = bf16[1024,1344]{0,1:T(8,128)(2,1)} collective-permute-done((bf16[1024,1344]{0,1:T(8,128)(2,1)S(1)}, bf16[1024,1344]{0,1:T(8,128)(2,1)}, u32[]{:S(2)}, u32[]{:S(2)}) %collective-permute-start.6) | collective-permute-done | bytes 2752544 | tf_op jit(solution)/shard_map/ppermute | solution.py:21
  690.0 3.6 constant_dynamic-update-slice_fusion
  693.7 11.0 %multiply_reduce_fusion = (f32[512]{0:T(512)S(1)}, f32[512,1344]{0,1:T(8,128)}) fusion(bf16[4096,1344]{0,1:T(8,128)(2,1)} %constant_dynamic-update-slice_fusion, bf16[512,4096]{0,1:T(8,128)(2,1)} %all-gather.14.cloned.1.call-done), kind=kOutput, calls=%fused_computation.20 | convolution fusion | flops 5638520320 | bytes 17958912 | tf_op jit(solution)/shard_map/dot_general | solution.py:125
  704.7 5.6 psum.7
  (62 shorter events, 27.6 us)
Async XLA Ops:
  6.5 47.0 %all-gather.6.cloned.1.call-start = ((), (), s32[]{:S(2)}) async-start(), calls=%async_computation | async-start | bytes 6881280 | tf_op jit(solution)/shard_map/all_gather | solution.py:63
  7.3 156.4 %all-gather.10.cloned.1.call-start = ((), (), s32[]{:S(2)}) async-start(), calls=%async_computation.2 | async-start | bytes 6881280 | tf_op jit(solution)/shard_map/all_gather | solution.py:71
  8.0 277.1 %all-gather.8.cloned.1.call-start = ((), (), s32[]{:S(2)}) async-start(), calls=%async_computation.1 | async-start | bytes 6881280 | tf_op jit(solution)/shard_map/all_gather | solution.py:72
  8.7 490.5 %all-gather.12.cloned.1.call-start = ((), (), s32[]{:S(2)}) async-start(), calls=%async_computation.3 | async-start | bytes 13762560 | tf_op jit(solution)/shard_map/all_gather | solution.py:70
  9.3 154.4 %copy-start.6 = (f32[5376]{0:T(1024)S(1)}, f32[5376]{0:T(1024)}, u32[]{:S(2)}) copy-start(f32[5376]{0:T(1024)} %param.10) | copy-start | bytes 64516
  9.3 684.3 %all-gather.14.cloned.1.call-start = ((), (), s32[]{:S(2)}) async-start(), calls=%async_computation.4 | async-start | bytes 5242880 | tf_op jit(solution)/shard_map/all_gather | solution.py:124
  9.4 543.6 %collective-permute-start.4 = (bf16[1024,1344]{0,1:T(8,128)(2,1)}, bf16[1024,1344]{0,1:T(8,128)(2,1)}, u32[]{:S(2)}, u32[]{:S(2)}) collective-permute-start(bf16[1024,1344]{0,1:T(8,128)(2,1)} %param.16), channel_id=1, source_target_pairs={{0,4},{4,8},{8,12},{12,0},{1,5},{5,9},{9,13},{13,1},{2,6},{6,10},{... | collective-permute-start | bytes 8257544 | tf_op jit(solution)/shard_map/ppermute | solution.py:21
  57.3 114.3 %copy-start.4 = (f32[128]{0:T(128)S(1)}, f32[128]{0:T(128)}, u32[]{:S(2)}) copy-start(f32[128]{0:T(128)} %param.15) | copy-start | bytes 1540
  173.0 143.3 %collective-permute-start.2 = (bf16[512,512]{0,1:T(8,128)(2,1)S(1)}, bf16[512,512]{0,1:T(8,128)(2,1)S(1)}, u32[]{:S(2)}, u32[]{:S(2)}) collective-permute-start(bf16[512,512]{0,1:T(8,128)(2,1)S(1)} %bitcast.55), channel_id=1, source_target_pairs={{0,8},{4,12},{1,9},{5,13},{2,10},{6,14},{3,11},{7,15},{16,24},{20,... | collective-permute-start | bytes 1572872 | tf_op jit(solution)/shard_map/ppermute | solution.py:28
  175.5 141.7 %collective-permute-start.3 = (bf16[512,512]{0,1:T(8,128)(2,1)S(1)}, bf16[512,512]{0,1:T(8,128)(2,1)S(1)}, u32[]{:S(2)}, u32[]{:S(2)}) collective-permute-start(bf16[512,512]{0,1:T(8,128)(2,1)S(1)} %bitcast.56), channel_id=1, source_target_pairs={{0,4},{4,8},{8,12},{1,5},{5,9},{9,13},{2,6},{6,10},{10,14},{3,7},{... | collective-permute-start | bytes 1572872 | tf_op jit(solution)/shard_map/ppermute | solution.py:28
  292.5 25.8 %collective-permute-start = (bf16[512,512]{1,0:T(8,128)(2,1)S(1)}, bf16[512,512]{1,0:T(8,128)(2,1)}, u32[]{:S(2)}, u32[]{:S(2)}) collective-permute-start(bf16[512,512]{1,0:T(8,128)(2,1)S(1)} %convolution_convert_fusion), channel_id=1, source_target_pairs={{0,8},{4,12},{1,9},{5,13},{2,10},{6,14},{3,11},{7,15},{16,24},{20,... | collective-permute-start | bytes 1572872 | tf_op jit(solution)/shard_map/ppermute | solution.py:28
  297.6 38.6 %collective-permute-start.1 = (bf16[512,512]{1,0:T(8,128)(2,1)S(1)}, bf16[512,512]{1,0:T(8,128)(2,1)}, u32[]{:S(2)}, u32[]{:S(2)}) collective-permute-start(bf16[512,512]{1,0:T(8,128)(2,1)S(1)} %convolution_convert_fusion), channel_id=1, source_target_pairs={{0,4},{4,8},{8,12},{1,5},{5,9},{9,13},{2,6},{6,10},{10,14},{3,7},{... | collective-permute-start | bytes 1572872 | tf_op jit(solution)/shard_map/ppermute | solution.py:28
  510.9 1.4 copy-start.5
  514.2 1.0 copy-start.1
  514.2 1.2 copy-start.2
  553.0 74.1 %collective-permute-start.5 = (bf16[1024,1344]{0,1:T(8,128)(2,1)}, bf16[1024,1344]{0,1:T(8,128)(2,1)S(1)}, u32[]{:S(2)}, u32[]{:S(2)}) collective-permute-start(bf16[1024,1344]{0,1:T(8,128)(2,1)} %collective-permute-done.4), channel_id=1, source_target_pairs={{0,4},{4,8},{8,12},{12,0},{1,5},{5,9},{9,13},{13,1},{2,6},{6,10},{... | collective-permute-start | bytes 8257544 | tf_op jit(solution)/shard_map/ppermute | solution.py:21
  627.1 62.9 %collective-permute-start.6 = (bf16[1024,1344]{0,1:T(8,128)(2,1)S(1)}, bf16[1024,1344]{0,1:T(8,128)(2,1)}, u32[]{:S(2)}, u32[]{:S(2)}) collective-permute-start(bf16[1024,1344]{0,1:T(8,128)(2,1)S(1)} %collective-permute-done.5), channel_id=1, source_target_pairs={{0,4},{4,8},{8,12},{12,0},{1,5},{5,9},{9,13},{13,1},{2,6},{6,10},{... | collective-permute-start | bytes 8257544 | tf_op jit(solution)/shard_map/ppermute | solution.py:21
  693.6 16.7 %copy-start = (bf16[512,1344]{0,1:T(8,128)(2,1)S(1)}, bf16[512,1344]{0,1:T(8,128)(2,1)}, u32[]{:S(2)}) copy-start(bf16[512,1344]{0,1:T(8,128)(2,1)} %param.9) | copy-start | bytes 4128772
  693.6 16.7 %copy-start.3 = (f32[1344]{0:T(1024)S(1)}, f32[1344]{0:T(1024)}, u32[]{:S(2)}) copy-start(f32[1344]{0:T(1024)} %param.17) | copy-start | bytes 16132
Sparse Core Ops, SparseCore 0:
  8.9 44.6 all-gather.5
  55.1 108.5 all-gather.9
  165.3 119.7 all-gather.7
  286.5 212.6 all-gather.11
  553.1 46.2 all-gather.13
